TPU v7x, 256 devices: a whole 4x4x8 slice. The times are simulated.
256 devices in a mesh: row: 16 (over x_lo, y, core), col: 16 (over z, x_hi).
Axes of the slice: x: 4 (x_hi: 2, x_lo: 2; x = x_hi * 2 + x_lo), y: 4, z: 8, core: 2. Of those that a mesh axis runs over, the one named last changes fastest.
Arguments:
- block_vecs: float32 [16, 131072], P(None, ('col', 'row')), may hold values from -130 to 130
- direction: float32 [16, 131072], P(None, ('col', 'row')), may hold values from -130 to 130
- blocks: bfloat16 [1024, 32, 128, 128], P('col', 'row'), may hold values from 0 to 4
- block_cols: int32 [1024, 32], P('col', 'row'), may hold values from 0 to 1023, as said below
- live_counts: int32 [1024, 16], P('col', 'row'), may hold values from 1 to 2, as said below
Outputs:
- x_next: float32 [16, 131072], P(None, ('col', 'row'))
- reduced: float32 [48, 48], replicated
- residual: float32 [16, 131072], P(None, ('col', 'row'))
Inputs may be any that keep to these rules, and one draw needn't show every extreme that they name: `block_cols`: A block column index g in slots 2 * r to 2 * r + 1 of any block row satisfies (g // 4) mod 16 == r. `live_counts`: every block row has 2 live slots in at least one segment.
All inputs are finite; a program needn't handle non-finite values.
Results may differ from a plain program's by a relative error of at most 0.0003.
Values sent between devices are 32-bit elements; how exact they have to be, the bound alone decides.
A program may use at most 64 MiB of HBM per device.

v0:
```python
import math

import jax
import jax.numpy as jnp
from jax import lax
from jax.sharding import PartitionSpec as P

highest = lax.Precision.HIGHEST


def outer(left, right):
    return jnp.dot(left, right.T, precision=highest, preferred_element_type=jnp.float32)


def cholesky_lower(matrix):
    order_small = matrix.shape[0]
    places = jnp.arange(order_small, dtype=jnp.int32)

    def column_step(step, lower):
        pick = (places == step).astype(jnp.float32)
        row_now = jnp.sum(lower * pick[:, None], axis=0)
        column_now = jnp.sum(matrix * pick[None, :], axis=1)
        pivot = jnp.sum(column_now * pick) - jnp.sum(row_now * row_now)
        pivot_root = jnp.sqrt(pivot)
        below = (column_now - jnp.sum(lower * row_now[None, :], axis=1)) / pivot_root
        values = jnp.where(places > step, below, jnp.where(places == step, pivot_root, 0.0))
        return lower + values[:, None] * pick[None, :]

    return lax.fori_loop(0, order_small, column_step, jnp.zeros_like(matrix))


def solve_lower(lower, right):
    order_small = lower.shape[0]
    places = jnp.arange(order_small, dtype=jnp.int32)

    def row_step(step, solved):
        pick = (places == step).astype(jnp.float32)
        row_now = jnp.sum(lower * pick[:, None], axis=0)
        pivot = jnp.sum(row_now * pick)
        right_row = jnp.sum(right * pick[:, None], axis=0)
        value = (right_row - jnp.sum(row_now[:, None] * solved, axis=0)) / pivot
        return solved + pick[:, None] * value[None, :]

    return lax.fori_loop(0, order_small, row_step, jnp.zeros_like(right))


def solve_upper_t(lower, right):
    order_small = lower.shape[0]
    places = jnp.arange(order_small, dtype=jnp.int32)

    def row_step(count, solved):
        step = order_small - 1 - count
        pick = (places == step).astype(jnp.float32)
        column_now = jnp.sum(lower * pick[None, :], axis=1)
        pivot = jnp.sum(column_now * pick)
        right_row = jnp.sum(right * pick[:, None], axis=0)
        value = (right_row - jnp.sum(column_now[:, None] * solved, axis=0)) / pivot
        return solved + pick[:, None] * value[None, :]

    return lax.fori_loop(0, order_small, row_step, jnp.zeros_like(right))


def local_layout(block_cols, live_counts, span_rows, block_size, row_count):
    per_span = span_rows // block_size
    span_index = block_cols // per_span
    local_cols = span_index // row_count * per_span + block_cols % per_span
    slot_count = block_cols.shape[1]
    live_mask = (jnp.arange(slot_count, dtype=jnp.int32)[None, :] < live_counts).astype(jnp.float32)
    return (local_cols, live_mask)


def forward_part(col_panel, blocks, local_cols, live_mask):
    vec_width = col_panel.shape[0]
    block_size = blocks.shape[2]
    col_blocks = col_panel.reshape(vec_width, -1, block_size)
    picked = col_blocks[:, local_cols, :] * live_mask[None, :, :, None]
    forward = jnp.einsum(
        "vbkj,bkij->vbi", picked, blocks, precision=highest, preferred_element_type=jnp.float32
    )
    return 0.5 * forward.reshape(vec_width, -1)


def backward_part(row_panel, col_length, blocks, local_cols, live_mask):
    vec_width = row_panel.shape[0]
    block_size = blocks.shape[2]
    row_blocks = row_panel.reshape(vec_width, -1, block_size)
    backward = (
        jnp.einsum(
            "vbi,bkij->vbkj",
            row_blocks,
            blocks,
            precision=highest,
            preferred_element_type=jnp.float32,
        )
        * live_mask[None, :, :, None]
    )
    spread = jnp.zeros((vec_width, col_length // block_size, block_size), jnp.float32)
    spread = spread.at[:, local_cols.reshape(-1), :].add(
        backward.reshape(vec_width, -1, block_size)
    )
    return 0.5 * spread.reshape(vec_width, -1)


def per_device(block_vecs, direction, blocks, block_cols, live_counts):
    row_count = lax.axis_size("row")
    col_count = lax.axis_size("col")
    vec_width = block_vecs.shape[0]
    span_rows = block_vecs.shape[1]
    order_total = span_rows * row_count * col_count
    col_length = span_rows * col_count
    block_size = blocks.shape[2]
    local_cols, live_mask = local_layout(block_cols, live_counts, span_rows, block_size, row_count)
    paired = jnp.concatenate([block_vecs, direction], axis=0)
    pair_cols = lax.all_gather(paired, "col", axis=1, tiled=True)
    pair_rows = lax.all_gather(paired, "row", axis=1, tiled=True)
    forward = forward_part(pair_cols, blocks, local_cols, live_mask)
    backward = backward_part(pair_rows, col_length, blocks, local_cols, live_mask)
    image_pair = lax.psum_scatter(
        forward, "row", scatter_dimension=1, tiled=True
    ) + lax.psum_scatter(backward, "col", scatter_dimension=1, tiled=True)
    image_x = image_pair[:vec_width]
    image_p = image_pair[vec_width:]
    gram_x, cross_x = lax.psum(
        (outer(block_vecs, block_vecs), outer(block_vecs, image_x)), ("row", "col")
    )
    factor_x = cholesky_lower(gram_x)
    coefficient = solve_upper_t(factor_x, solve_lower(factor_x, cross_x))
    resid = image_x - jnp.dot(
        coefficient.T, block_vecs, precision=highest, preferred_element_type=jnp.float32
    )
    basis = jnp.concatenate([block_vecs, resid, direction], axis=0)
    resid_cols = lax.all_gather(resid, "col", axis=1, tiled=True)
    resid_rows = lax.all_gather(resid, "row", axis=1, tiled=True)
    forward_r = forward_part(resid_cols, blocks, local_cols, live_mask)
    column_x = outer(basis, image_x)
    column_p = outer(basis, image_p)
    backward_r = backward_part(resid_rows, col_length, blocks, local_cols, live_mask)
    image_r = lax.psum_scatter(
        forward_r, "row", scatter_dimension=1, tiled=True
    ) + lax.psum_scatter(backward_r, "col", scatter_dimension=1, tiled=True)
    column_r = outer(basis, image_r)
    gram_apply = jnp.concatenate([column_x, column_r, column_p], axis=1)
    gram_basis, gram_apply = lax.psum((outer(basis, basis), gram_apply), ("row", "col"))
    factor = cholesky_lower(gram_basis)
    halfway = solve_lower(factor, 0.5 * (gram_apply + gram_apply.T))
    reduced = solve_lower(factor, halfway.T)
    shifted = reduced + 3.0 * jnp.eye(3 * vec_width, dtype=jnp.float32)
    target = jnp.dot(
        shifted, shifted[:, :vec_width], precision=highest, preferred_element_type=jnp.float32
    )
    mixing = solve_upper_t(factor, target)
    fresh = jnp.dot(mixing.T, basis, precision=highest, preferred_element_type=jnp.float32)
    gram_fresh = lax.psum(outer(fresh, fresh), ("row", "col"))
    factor_fresh = cholesky_lower(gram_fresh)
    x_next = math.sqrt(order_total) * solve_lower(factor_fresh, fresh)
    return (x_next, reduced, resid)


def solution(mesh):
    return jax.shard_map(
        per_device,
        mesh=mesh,
        in_specs=(
            P(None, ("col", "row")),
            P(None, ("col", "row")),
            P("col", "row", None, None),
            P("col", "row"),
            P("col", "row"),
        ),
        out_specs=(P(None, ("col", "row")), P(), P(None, ("col", "row"))),
        check_vma=False,
    )
```

profile of v0, /device:TPU:1, one launch (start us, length us, event | category | flops | bytes accessed | tf_op | source)
XLA Modules:
  0.0 1421.3 jit_solution(11187509048310806808)
XLA Ops:
  11.9 37.2 %all-gather.5.cloned.1.call-done = f32[32,8192]{1,0:T(8,128)} async-done(((f32[32,512]{1,0:T(8,128)}), f32[32,8192]{1,0:T(8,128)}) %all-gather.5.cloned.1.call-update) | async-done | bytes 1048592 | tf_op jit(solution)/shard_map/all_gather | solution.py:115
  54.9 5.7 scatter_fusion
  62.0 64.4 %all-gather.3.cloned.1.call-done = f32[32,8192]{1,0:T(8,128)} async-done(((f32[32,512]{1,0:T(8,128)}), f32[32,8192]{1,0:T(8,128)}) %all-gather.3.cloned.1.call-update) | async-done | bytes 1048592 | tf_op jit(solution)/shard_map/all_gather | solution.py:114
  128.6 6.0 fusion.45
  135.9 192.4 %reduce-scatter.7.cloned.1.call-done = f32[32,512]{1,0:T(8,128)} async-done(((f32[32,8192]{1,0:T(8,128)}), f32[32,512]{1,0:T(8,128)}) %reduce-scatter.7.cloned.1.call-update) | async-done | bytes 65552 | tf_op jit(solution)/shard_map/reduce_scatter | solution.py:120
  328.3 66.4 %reduce-scatter.5.cloned.1.call-done = f32[32,512]{1,0:T(8,128)} async-done(((f32[32,8192]{1,0:T(8,128)}), f32[32,512]{1,0:T(8,128)}) %reduce-scatter.5.cloned.1.call-update) | async-done | bytes 65552 | tf_op jit(solution)/shard_map/reduce_scatter | solution.py:118
  395.7 78.8 %all-reduce.1 = (f32[16,16]{0,1:T(8,128)S(1)}, f32[16,16]{1,0:T(8,128)S(1)}) all-reduce(f32[16,16]{0,1:T(8,128)S(1)} %convolution_bitcast_fusion.1, f32[16,16]{1,0:T(8,128)S(1)} %fusion.72), channel_id=1, replica_groups=mesh['row'=16,'col'=16] {'row','col'}, use_global_device_ids=true, to_apply=%region_11.12 | all-reduce | flops 512 | bytes 4096 | tf_op jit(solution)/shard_map/psum | solution.py:123
  474.5 37.0 %while.135 = (s32[]{:T(128)}, f32[16,16]{1,0:T(8,128)S(1)}, f32[16,16]{1,0:T(8,128)S(1)}, s32[]{:T(128)}, s32[]{:T(128)}) while((s32[]{:T(128)}, f32[16,16]{1,0:T(8,128)S(1)}, f32[16,16]{1,0:T(8,128)S(1)}, s32[]{:T(128)}, s32[]{:T(128)}) %tuple.302), condition=%wide.region_10.11_spmd.clone.clone, body=%wide.region_4.10_spmd.clone.clone.sunk | while | flops 2978 | bytes 6069 | solution.py:29
  511.6 24.3 %while.129 = (s32[]{:T(128)}, f32[16,16]{1,0:T(8,128)S(1)}, f32[16,16]{1,0:T(8,128)S(1)}, f32[16,16]{1,0:T(8,128)S(1)}, s32[]{:T(128)}, /*index=5*/s32[]{:T(128)}) while((s32[]{:T(128)}, f32[16,16]{1,0:T(8,128)S(1)}, f32[16,16]{1,0:T(8,128)S(1)}, f32[16,16]{1,0:T(8,128)S(1)}, s32[]{:T(128)}, /*index=5*/s32[]{:T(128)}) %tuple.305), condition=%wide.region_17.18_spmd.clone, body=%wide.region_12.17_spmd.clone.sunk | while | flops 2626 | bytes 5984 | solution.py:44
  535.9 24.8 %while.130 = (s32[]{:T(128)}, f32[16,16]{1,0:T(8,128)S(1)}, f32[16,16]{1,0:T(8,128)S(1)}, f32[16,16]{1,0:T(8,128)S(1)}, s32[]{:T(128)}, /*index=5*/s32[]{:T(128)}, s32[]{:T(128)}) while((s32[]{:T(128)}, f32[16,16]{1,0:T(8,128)S(1)}, f32[16,16]{1,0:T(8,128)S(1)}, f32[16,16]{1,0:T(8,128)S(1)}, s32[]{:T(128)}, ...), condition=%wide.region_23.24_spmd.clone, body=%wide.region_18.23_spmd.clone.sunk | while | flops 2627 | bytes 6004 | solution.py:60
  560.9 19.6 %all_gather.15 = f32[16,8192]{1,0:T(8,128)S(1)} all-gather(f32[16,512]{1,0:T(8,128)S(1)} %convolution_subtract_fusion), channel_id=1, replica_groups=mesh['row'=16,'col'=16] {'row'}, dimensions={1}, use_global_device_ids=true | all-gather | bytes 557056 | tf_op jit(solution)/shard_map/all_gather | solution.py:133
  584.5 5.2 scatter_fusion.1
  590.6 34.6 %all_gather.14 = f32[16,8192]{1,0:T(8,128)S(1)} all-gather(f32[16,512]{1,0:T(8,128)S(1)} %convolution_subtract_fusion), channel_id=1, replica_groups=mesh['row'=16,'col'=16] {'col'}, dimensions={1}, use_global_device_ids=true | all-gather | bytes 557056 | tf_op jit(solution)/shard_map/all_gather | solution.py:132
  626.0 5.2 fusion.49
  632.8 145.3 %reduce-scatter.11.cloned.1.call-done = f32[16,512]{1,0:T(8,128)} async-done(((f32[16,8192]{1,0:T(8,128)}), f32[16,512]{1,0:T(8,128)}) %reduce-scatter.11.cloned.1.call-update) | async-done | bytes 32784 | tf_op jit(solution)/shard_map/reduce_scatter | solution.py:140
  778.1 65.7 %reduce-scatter.9.cloned.1.call-done = f32[16,512]{1,0:T(8,128)} async-done(((f32[16,8192]{1,0:T(8,128)}), f32[16,512]{1,0:T(8,128)}) %reduce-scatter.9.cloned.1.call-update) | async-done | bytes 32784 | tf_op jit(solution)/shard_map/reduce_scatter | solution.py:138
  844.8 79.4 %all-reduce = (f32[48,48]{0,1:T(8,128)S(1)}, f32[48,48]{1,0:T(8,128)S(1)}) all-reduce(f32[48,48]{0,1:T(8,128)S(1)} %pad_maximum_fusion.1, f32[48,48]{1,0:T(8,128)S(1)} %fusion.70), channel_id=1, replica_groups=mesh['row'=16,'col'=16] {'row','col'}, use_global_device_ids=true, to_apply=%region_35.36 | all-reduce | flops 4608 | bytes 36864 | tf_op jit(solution)/shard_map/psum | solution.py:143
  924.3 111.3 %while.136 = (s32[]{:T(128)}, f32[48,48]{1,0:T(8,128)S(1)}, f32[48,48]{1,0:T(8,128)S(1)}, s32[]{:T(128)}, s32[]{:T(128)}) while((s32[]{:T(128)}, f32[48,48]{1,0:T(8,128)S(1)}, f32[48,48]{1,0:T(8,128)S(1)}, s32[]{:T(128)}, s32[]{:T(128)}) %tuple.311), condition=%wide.region_31.32_spmd.clone.clone, body=%wide.region_25.31_spmd.clone.clone.sunk | while | flops 25826 | bytes 48693 | solution.py:29
  1035.6 79.4 %while.131 = (s32[]{:T(128)}, f32[48,48]{1,0:T(8,128)S(1)}, f32[48,48]{1,0:T(8,128)S(1)}, f32[48,48]{1,0:T(8,128)S(1)}, s32[]{:T(128)}, /*index=5*/s32[]{:T(128)}) while((s32[]{:T(128)}, f32[48,48]{1,0:T(8,128)S(1)}, f32[48,48]{1,0:T(8,128)S(1)}, f32[48,48]{1,0:T(8,128)S(1)}, s32[]{:T(128)}, /*index=5*/s32[]{:T(128)}) %tuple.314), condition=%wide.region_41.42_spmd.clone, body=%wide.region_36.41_spmd.clone.sunk | while | flops 23234 | bytes 48480 | solution.py:44
  1115.1 79.4 %while.132 = (s32[]{:T(128)}, f32[48,48]{1,0:T(8,128)S(1)}, f32[48,48]{1,0:T(8,128)S(1)}, f32[48,48]{1,0:T(8,128)S(1)}, s32[]{:T(128)}, /*index=5*/s32[]{:T(128)}) while((s32[]{:T(128)}, f32[48,48]{1,0:T(8,128)S(1)}, f32[48,48]{1,0:T(8,128)S(1)}, f32[48,48]{1,0:T(8,128)S(1)}, s32[]{:T(128)}, /*index=5*/s32[]{:T(128)}) %tuple.344), condition=%wide.region_47.48_spmd.clone, body=%wide.region_42.47_spmd.clone.sunk | while | flops 23234 | bytes 48480 | solution.py:44
  1194.7 81.8 %while.133 = (s32[]{:T(128)}, f32[48,16]{0,1:T(8,128)S(1)}, f32[48,16]{0,1:T(8,128)S(1)}, f32[48,48]{1,0:T(8,128)S(1)}, s32[]{:T(128)}, /*index=5*/s32[]{:T(128)}, s32[]{:T(128)}) while((s32[]{:T(128)}, f32[48,16]{0,1:T(8,128)S(1)}, f32[48,16]{0,1:T(8,128)S(1)}, f32[48,48]{1,0:T(8,128)S(1)}, s32[]{:T(128)}, ...), condition=%wide.region_53.54_spmd.clone, body=%wide.region_48.53_spmd.clone.sunk | while | flops 10947 | bytes 23348 | solution.py:60
  1276.8 73.6 %psum.39 = f32[16,16]{1,0:T(8,128)S(1)} all-reduce(f32[16,16]{1,0:T(8,128)S(1)} %fusion.73), channel_id=1, replica_groups=mesh['row'=16,'col'=16] {'row','col'}, use_global_device_ids=true, to_apply=%region_54.55 | all-reduce | flops 256 | bytes 2048 | tf_op jit(solution)/shard_map/psum | solution.py:153
  1350.5 37.0 %while.137 = (s32[]{:T(128)}, f32[16,16]{1,0:T(8,128)S(1)}, f32[16,16]{1,0:T(8,128)S(1)}, s32[]{:T(128)}, s32[]{:T(128)}) while((s32[]{:T(128)}, f32[16,16]{1,0:T(8,128)S(1)}, f32[16,16]{1,0:T(8,128)S(1)}, s32[]{:T(128)}, s32[]{:T(128)}) %tuple.323), condition=%wide.region_61.62_spmd.clone.clone, body=%wide.region_55.61_spmd.clone.clone.sunk | while | flops 2978 | bytes 6069 | solution.py:29
  1387.5 26.3 %while.134 = (s32[]{:T(128)}, f32[16,512]{1,0:T(8,128)S(1)}, f32[16,512]{1,0:T(8,128)S(1)}, f32[16,16]{1,0:T(8,128)S(1)}, s32[]{:T(128)}, /*index=5*/s32[]{:T(128)}) while((s32[]{:T(128)}, f32[16,512]{1,0:T(8,128)S(1)}, f32[16,512]{1,0:T(8,128)S(1)}, f32[16,16]{1,0:T(8,128)S(1)}, s32[]{:T(128)}, /*index=5*/s32[]{:T(128)}) %tuple.326), condition=%wide.region_67.68_spmd.clone, body=%wide.region_62.67_spmd.clone.sunk | while | flops 66114 | bytes 144928 | solution.py:44
  (1706 shorter events, 420.2 us)
Async XLA Ops:
  7.2 41.9 %all-gather.5.cloned.1.call-start = ((), (), s32[]{:S(2)}) async-start(), calls=%async_computation.6 | async-start | bytes 1114112 | tf_op jit(solution)/shard_map/all_gather | solution.py:115
  8.7 0.6 copy-start.4
  9.4 117.1 %all-gather.3.cloned.1.call-start = ((), (), s32[]{:S(2)}) async-start(), calls=%async_computation.4 | async-start | bytes 1114112 | tf_op jit(solution)/shard_map/all_gather | solution.py:114
  10.1 318.2 %reduce-scatter.7.cloned.1.call-start = ((), (), s32[]{:S(2)}) async-start(), calls=%async_computation.7 | async-start | bytes 1114112 | tf_op jit(solution)/shard_map/reduce_scatter | solution.py:120
  61.7 333.0 %reduce-scatter.5.cloned.1.call-start = ((), (), s32[]{:S(2)}) async-start(), calls=%async_computation.5 | async-start | bytes 1114112 | tf_op jit(solution)/shard_map/reduce_scatter | solution.py:118
  134.6 1.2 copy-start.1
  135.7 642.4 %reduce-scatter.11.cloned.1.call-start = ((), (), s32[]{:S(2)}) async-start(), calls=%async_computation.9 | async-start | bytes 557056 | tf_op jit(solution)/shard_map/reduce_scatter | solution.py:140
  560.9 715.6 %copy-start.2 = (f32[16,512]{1,0:T(8,128)}, f32[16,512]{1,0:T(8,128)S(1)}, u32[]{:S(2)}) copy-start(f32[16,512]{1,0:T(8,128)S(1)} %convolution_subtract_fusion) | copy-start | bytes 98308
  590.5 253.2 %reduce-scatter.9.cloned.1.call-start = ((), (), s32[]{:S(2)}) async-start(), calls=%async_computation.8 | async-start | bytes 557056 | tf_op jit(solution)/shard_map/reduce_scatter | solution.py:138
  626.0 6.1 copy-start.3
  1194.5 219.9 %copy-start = (f32[48,48]{1,0:T(8,128)}, f32[48,48]{1,0:T(8,128)S(1)}, u32[]{:S(2)}) copy-start(f32[48,48]{1,0:T(8,128)S(1)} %get-tuple-element.811) | copy-start | bytes 27652
Sparse Core Ops, SparseCore 0:
  9.8 39.1 all-gather.4
  51.6 74.7 all-gather.2
  130.3 198.0 reduce-scatter.6
  330.7 63.9 reduce-scatter.4
  590.7 187.3 reduce-scatter.10
  780.4 63.2 reduce-scatter.8
where the time goes:
time: 1430 us; the launch traced here: 1420 us
  waiting for transfers between devices  572 us (40%)
  other arithmetic  410 us (29%)
  blocking collectives  286 us (20%)
  loops' own time  107 us (7%)
  matrix products  21.8 us (2%)
  between operations  14.4 us (1%)
    reduce_scatter x1, waiting for transfers between devices, per_device(): lax.psum_scatter(backward, 'col', scatter_dimension=1, tiled=True)  192 us
    reduce_scatter x1, waiting for transfers between devices, per_device(): lax.psum_scatter(backward_r, 'col', scatter_dimension=1, tiled=True)  145 us
    another operation x3, loops' own time, cholesky_lower(): return lax.fori_loop(0, order_small, column_step, jnp.zeros_like(matrix))  105 us
    div x128, other arithmetic, row_step(): value = (right_row - jnp.sum(row_now[:, None] * solved, axis=0)) / pivot  87.9 us
    reduce_sum x128, other arithmetic, row_step(): pivot = jnp.sum(row_now * pick)  85.7 us
    psum x1, blocking collectives, per_device(): lax.psum((outer(basis, basis), gram_apply), ('row', 'col'))  79.4 us
    psum x1, blocking collectives, per_device(): lax.psum((outer(block_vecs, block_vecs), outer(block_vecs, image_x)), ('r...  78.8 us
    psum x1, blocking collectives, per_device(): gram_fresh = lax.psum(outer(fresh, fresh), ('row', 'col'))  73.6 us
  transfers between devices with their start and end apart: 6, of which 6 were waited for; matrix products, arithmetic and copies ran while one was open for 2% of the time, Pallas kernels for 0%

commit v1 on v0

v1 whole, which is shorter than its diff:
```python
import functools
import math

import jax
import jax.numpy as jnp
from jax import lax
from jax.experimental import pallas as pl
from jax.experimental.pallas import tpu as pltpu
from jax.sharding import PartitionSpec as P

MESH = pl.DeviceIdType.MESH
F32 = jnp.float32
BF16 = jnp.bfloat16
LANES = 128
NT = (((1,), (1,)), ((), ()))
NN = (((1,), (0,)), ((), ()))

AG1_ROW, AG1_COL, RS1_ROW, RS1_COL = 0, 1, 2, 3
AG2_ROW, AG2_COL, RS2_ROW, RS2_COL = 4, 5, 6, 7
AR1_ROW, AR1_COL, AR2_ROW, AR2_COL, AR3_ROW, AR3_COL = 8, 9, 10, 11, 12, 13
STAGES = 14


def mm(left, right, dims=NN):
    return lax.dot_general(
        left, right, dims, precision=lax.Precision.HIGHEST, preferred_element_type=F32
    )


def fast_mm(left, right, dims=NN):
    return lax.dot_general(left, right, dims, preferred_element_type=F32)


def split_rows(value):
    high = value.astype(BF16)
    low = (value - high.astype(F32)).astype(BF16)
    return jnp.concatenate([high, low], axis=0)


def pad_rows(value, rows):
    return jnp.concatenate(
        [value, jnp.zeros((rows - value.shape[0], value.shape[1]), value.dtype)], axis=0
    )


def lanes_of(rows):
    return lax.broadcasted_iota(jnp.int32, (rows, LANES), 1)


def subs_of(rows):
    return lax.broadcasted_iota(jnp.int32, (rows, LANES), 0)


def eliminate(work, order):
    lane, sub = lanes_of(order), subs_of(order)

    def step(k, work):
        row = jnp.sum(jnp.where(sub == k, work, 0.0), axis=0, keepdims=True)
        col = jnp.sum(jnp.where(lane == k, work, 0.0), axis=1, keepdims=True)
        pivot = jnp.sum(jnp.where(lane[:1] == k, row, 0.0), axis=1, keepdims=True)
        inverse = 1.0 / jnp.sqrt(pivot)
        row = row * inverse
        col = col * inverse
        return jnp.where(sub == k, row, jnp.where(sub > k, work - col * row, work))

    return lax.fori_loop(0, order, step, work)


def step_kernel(
    n_row,
    n_col,
    x_ref,
    p_ref,
    blocks_hbm,
    cols_s,
    live_s,
    cols_v,
    live_v,
    next_ref,
    reduced_ref,
    resid_ref,
    blk,
    rp1,
    cp1,
    g1,
    fs1,
    bs1,
    fr1,
    br1,
    rp2,
    cp2,
    g2,
    fs2,
    bs2,
    fr2,
    br2,
    ar1r,
    ar1c,
    ar2r,
    ar2c,
    ar3r,
    ar3c,
    send_sem,
    recv_sem,
    blk_sem,
):
    me_r = lax.axis_index("row")
    me_c = lax.axis_index("col")
    width, span = x_ref.shape
    per = span // LANES
    nb = blocks_hbm.shape[0]
    ncb = per * n_col
    slots = 2 * nb
    order_total = span * n_row * n_col
    sizes = {"row": n_row, "col": n_col}
    mine = {"row": me_r, "col": me_c}

    def copy_to(axis, stage, src, dst, peer):
        return pltpu.make_async_remote_copy(
            src_ref=src,
            dst_ref=dst,
            send_sem=send_sem.at[stage, peer],
            recv_sem=recv_sem.at[stage, mine[axis]],
            device_id={axis: peer},
            device_id_type=MESH,
        )

    def arrival(axis, stage, dst, source):
        return pltpu.make_async_remote_copy(
            src_ref=dst,
            dst_ref=dst,
            send_sem=send_sem.at[stage, source],
            recv_sem=recv_sem.at[stage, source],
            device_id={axis: source},
            device_id_type=MESH,
        )

    def over_peers(axis, body, carry=0):
        n = sizes[axis]
        return lax.fori_loop(
            1, n, lambda d, c: body(lax.rem(mine[axis] + d, n), c), carry
        )

    def share(axis, stage, buf):
        own = buf.at[mine[axis]]

        def body(peer, c):
            copy_to(axis, stage, own, own, peer).start()
            return c

        over_peers(axis, body)

    def collect(axis, stage, buf):
        def body(source, c):
            arrival(axis, stage, buf.at[source], source).wait_recv()
            return c

        over_peers(axis, body)

    def drain(axis, stage, buf):
        def body(peer, c):
            copy_to(axis, stage, buf.at[mine[axis]], buf.at[mine[axis]], peer).wait_send()
            return c

        over_peers(axis, body)

    def total_of(buf, n):
        return lax.fori_loop(1, n, lambda i, t: t + buf[i], buf[0])

    def sum_begin(axis, stage, buf, value):
        buf[mine[axis]] = value
        share(axis, stage, buf)

    def sum_end(axis, stage, buf):
        collect(axis, stage, buf)
        return total_of(buf, sizes[axis])

    fetch = pltpu.make_async_copy(blocks_hbm, blk, blk_sem)
    fetch.start()
    barrier = pltpu.get_barrier_semaphore()
    for axis in ("row", "col"):

        def greet(peer, c, axis=axis):
            pl.semaphore_signal(
                barrier, inc=1, device_id={axis: peer}, device_id_type=MESH
            )
            return c

        over_peers(axis, greet)

    x_now = x_ref[...]
    p_now = p_ref[...]
    for o in range(per):
        piece = jnp.concatenate(
            [x_now[:, o * LANES : (o + 1) * LANES], p_now[:, o * LANES : (o + 1) * LANES]],
            axis=0,
        )
        rp1[me_r, o] = piece
        cp1[me_c, o] = piece
    pl.semaphore_wait(barrier, n_row + n_col - 2)

    share("col", AG1_COL, cp1)
    share("row", AG1_ROW, rp1)

    row_step = per * n_row
    hot = []
    for k in range(2):
        cols = cols_v[:, k : k + 1]
        place = cols // row_step * per + cols % per
        weight = jnp.where(live_v[...] > k, 0.5, 0.0)
        hot.append(
            jnp.where(lax.broadcasted_iota(jnp.int32, (nb, LANES), 1) == place, weight, 0.0)
        )
    hot = jnp.concatenate(hot, axis=0)
    if slots < LANES:
        hot = pad_rows(hot, LANES)
    hot = hot.T[:ncb, :slots].astype(BF16)
    hot = jnp.concatenate([hot, hot], axis=1)

    def pair_of(b):
        return jnp.concatenate([blk[b, 0], blk[b, 1]], axis=1)

    def backward(panel, prod, spread, v):
        def group(r, c):
            for o in range(per):
                b = r * per + o
                out = fast_mm(split_rows(panel[r, o]), pair_of(b))
                out = out[:v] + out[v:]
                for k in range(2):
                    start = pl.multiple_of((k * nb + b) * v, v)
                    prod[pl.ds(start, v), :] = out[:, k * LANES : (k + 1) * LANES]
            return c

        lax.fori_loop(0, n_row, group, 0)
        for vec in range(v):
            part = split_rows(prod[pl.ds(vec, slots, stride=v), :])
            spread[pl.ds(vec, ncb, stride=v), :] = fast_mm(hot, part)

    def spread_piece(spread, v, c):
        return spread.at[pl.ds(pl.multiple_of(c * per * v, per * v), per * v), :]

    def send_back(stage, spread, landed, v):
        def body(peer, c):
            copy_to("col", stage, spread_piece(spread, v, peer), landed.at[me_c], peer).start()
            return c

        over_peers("col", body)

    def forward_group(panel, out_buf, v, r):
        for o in range(per):
            b = r * per + o
            picked = []
            for k in range(2):
                g = cols_s[b, k]
                weight = jnp.where(live_s[b, 0] > k, 0.5, 0.0)
                picked.append(panel[g // row_step, g % per] * weight)
            out = fast_mm(split_rows(jnp.concatenate(picked, axis=1)), pair_of(b), NT)
            start = o * v
            out_buf[r, start : start + v, :] = out[:v] + out[v:]

    def forward(stage, panel, out_buf, landed, v):
        def body(peer, c):
            forward_group(panel, out_buf, v, peer)
            copy_to("row", stage, out_buf.at[peer], landed.at[me_r], peer).start()
            return c

        over_peers("row", body)
        forward_group(panel, out_buf, v, me_r)

    def gather_sum(stage_row, stage_col, fs, bs, fr, br, v):
        start = pl.multiple_of(me_c * per * v, per * v)
        total = fs[me_r] + bs[pl.ds(start, per * v), :]

        def row_body(source, t):
            arrival("row", stage_row, fr.at[source], source).wait_recv()
            return t + fr[source]

        total = over_peers("row", row_body, total)

        def col_body(source, t):
            arrival("col", stage_col, br.at[source], source).wait_recv()
            return t + br[source]

        return over_peers("col", col_body, total)

    def drain_apply(stage_row, stage_col, fs, bs, fr, br, v):
        def row_body(peer, c):
            copy_to("row", stage_row, fs.at[peer], fr.at[me_r], peer).wait_send()
            return c

        over_peers("row", row_body)

        def col_body(peer, c):
            copy_to("col", stage_col, spread_piece(bs, v, peer), br.at[me_c], peer).wait_send()
            return c

        over_peers("col", col_body)

    v1, v2 = 2 * width, width
    fetch.wait()
    collect("row", AG1_ROW, rp1)
    backward(rp1, g1, bs1, v1)
    send_back(RS1_COL, bs1, br1, v1)
    collect("col", AG1_COL, cp1)
    forward(RS1_ROW, cp1, fs1, fr1, v1)
    image = gather_sum(RS1_ROW, RS1_COL, fs1, bs1, fr1, br1, v1)

    image_x, image_p = [], []
    for o in range(per):
        top = image[o * v1 : o * v1 + width]
        image_x.append(top)
        image_p.append(image[o * v1 + width : (o + 1) * v1])
        rp2[me_r, o] = top
        cp2[me_c, o] = top
    share("col", AG2_COL, cp2)
    share("row", AG2_ROW, rp2)
    image_x = jnp.concatenate(image_x, axis=1)
    image_p = jnp.concatenate(image_p, axis=1)

    gap = jnp.zeros((width, span), F32)
    right = jnp.concatenate([x_now, gap, p_now, gap, image_x, gap, image_p, gap], axis=0)
    sum_begin("row", AR1_ROW, ar1r, mm(jnp.concatenate([x_now, p_now], axis=0), right, NT))

    collect("row", AG2_ROW, rp2)
    backward(rp2, g2, bs2, v2)
    send_back(RS2_COL, bs2, br2, v2)
    sum_begin("col", AR1_COL, ar1c, sum_end("row", AR1_ROW, ar1r))
    collect("col", AG2_COL, cp2)
    forward(RS2_ROW, cp2, fs2, fr2, v2)

    first = sum_end("col", AR1_COL, ar1c)
    row_x, row_p = first[:width], first[width:]
    lane, sub = lanes_of(width), subs_of(width)
    work = jnp.where((lane < width) | ((lane >= 64) & (lane < 64 + width)), row_x, 0.0)
    work = eliminate(work + jnp.where(lane == sub + 96, 1.0, 0.0), width)
    halfway = jnp.where(lane < width, pltpu.roll(work, 64, 1), 0.0)
    inverse = jnp.where(lane < width, pltpu.roll(work, 32, 1), 0.0)
    coef_t = mm(pad_rows(halfway, LANES).T[:width], pad_rows(inverse, LANES))
    moved = mm(coef_t, pad_rows(jnp.concatenate([x_now, image_x], axis=1), LANES))
    resid = image_x - moved[:, :span]
    resid_ref[...] = resid

    right = jnp.concatenate([x_now, resid, p_now, gap, image_x, gap, image_p, gap], axis=0)
    sum_begin("row", AR2_ROW, ar2r, mm(resid, right, NT))
    sum_begin("col", AR2_COL, ar2c, sum_end("row", AR2_ROW, ar2r))

    again = gather_sum(RS2_ROW, RS2_COL, fs2, bs2, fr2, br2, v2)
    again = jnp.concatenate([again[o * v2 : (o + 1) * v2] for o in range(per)], axis=1)
    image_r = again - moved[:, span:]
    sum_begin("row", AR3_ROW, ar3r, mm(image_r, right, NT))
    row_r = sum_end("col", AR2_COL, ar2c)
    sum_begin("col", AR3_COL, ar3c, sum_end("row", AR3_ROW, ar3r))

    full = 3 * width
    lane, sub = lanes_of(full), subs_of(full)
    rows = jnp.concatenate([row_x, row_r, row_p], axis=0)
    middle = (lane >= width) & (lane < 2 * width)
    outside = (sub < width) | (sub >= 2 * width)
    flipped = pad_rows(rows, LANES).T[:full]
    gram = jnp.where(lane < full, jnp.where(middle & outside, flipped, rows), 0.0)
    work = eliminate(gram + jnp.where(lane == sub + 64, 1.0, 0.0), full)
    inverse = jnp.where(lane < full, pltpu.roll(work, 64, 1), 0.0)
    inverse_pad = pad_rows(inverse, LANES)
    known = jnp.where((lane < full) & jnp.logical_not(middle), pltpu.roll(rows, 64, 1), 0.0)
    known = 0.5 * (known + pad_rows(known, LANES).T[:full])

    last = sum_end("col", AR3_COL, ar3c)
    last = jnp.where(lanes_of(width) < full, last, 0.0)
    edge = jnp.zeros((width, LANES), F32)
    last = jnp.concatenate([edge, last, edge], axis=0)
    middle_matrix = known + 0.5 * (last + pad_rows(last, LANES).T[:full])

    reduced = mm(mm(inverse, pad_rows(middle_matrix, LANES)), inverse_pad, NT)
    reduced_ref[...] = reduced[:, :full]
    shifted = reduced + jnp.where(lane == sub, 3.0, 0.0)
    target_t = mm(shifted[:width], pad_rows(shifted, LANES))
    mixing_t = mm(target_t, inverse_pad)
    gram_new = mm(target_t, pad_rows(target_t, LANES), NT)
    lane = lanes_of(width)
    work = jnp.where(lane < width, gram_new, 0.0) + pltpu.roll(mixing_t, 64, 1)
    work = eliminate(work, width)
    final = jnp.where(lane < full, pltpu.roll(work, 64, 1), 0.0) * math.sqrt(order_total)
    next_ref[...] = mm(final, pad_rows(jnp.concatenate([x_now, resid, p_now], axis=0), LANES))

    drain("row", AG1_ROW, rp1)
    drain("col", AG1_COL, cp1)
    drain("row", AG2_ROW, rp2)
    drain("col", AG2_COL, cp2)
    drain("row", AR1_ROW, ar1r)
    drain("col", AR1_COL, ar1c)
    drain("row", AR2_ROW, ar2r)
    drain("col", AR2_COL, ar2c)
    drain("row", AR3_ROW, ar3r)
    drain("col", AR3_COL, ar3c)
    drain_apply(RS1_ROW, RS1_COL, fs1, bs1, fr1, br1, v1)
    drain_apply(RS2_ROW, RS2_COL, fs2, bs2, fr2, br2, v2)


def per_device(block_vecs, direction, blocks, block_cols, live_counts):
    n_row = lax.axis_size("row")
    n_col = lax.axis_size("col")
    width, span = block_vecs.shape
    per = span // LANES
    nb = blocks.shape[0]
    v1, v2 = 2 * width, width
    vmem = pl.BlockSpec(memory_space=pltpu.VMEM)
    smem = pl.BlockSpec(memory_space=pltpu.SMEM)

    def panels(v):
        return [
            pltpu.VMEM((n_row, per, v, LANES), F32),
            pltpu.VMEM((n_col, per, v, LANES), F32),
            pltpu.VMEM((2 * nb * v, LANES), F32),
            pltpu.VMEM((n_row, per * v, LANES), F32),
            pltpu.VMEM((n_col * per * v, LANES), F32),
            pltpu.VMEM((n_row, per * v, LANES), F32),
            pltpu.VMEM((n_col, per * v, LANES), F32),
        ]

    sums = []
    for rows in (2 * width, width, width):
        sums += [pltpu.VMEM((n_row, rows, LANES), F32), pltpu.VMEM((n_col, rows, LANES), F32)]
    peers = max(n_row, n_col)
    return pl.pallas_call(
        functools.partial(step_kernel, n_row, n_col),
        out_shape=(
            jax.ShapeDtypeStruct((width, span), F32),
            jax.ShapeDtypeStruct((3 * width, 3 * width), F32),
            jax.ShapeDtypeStruct((width, span), F32),
        ),
        in_specs=[
            vmem,
            vmem,
            pl.BlockSpec(memory_space=pl.ANY),
            smem,
            smem,
            vmem,
            vmem,
        ],
        out_specs=(vmem, vmem, vmem),
        scratch_shapes=[
            pltpu.VMEM(blocks.shape, blocks.dtype),
            *panels(v1),
            *panels(v2),
            *sums,
            pltpu.SemaphoreType.DMA((STAGES, peers)),
            pltpu.SemaphoreType.DMA((STAGES, peers)),
            pltpu.SemaphoreType.DMA(()),
        ],
        compiler_params=pltpu.CompilerParams(
            collective_id=0, has_side_effects=True, vmem_limit_bytes=48 * 2**20
        ),
    )(block_vecs, direction, blocks, block_cols, live_counts, block_cols, live_counts)


def solution(mesh):
    return jax.shard_map(
        per_device,
        mesh=mesh,
        in_specs=(
            P(None, ("col", "row")),
            P(None, ("col", "row")),
            P("col", "row", None, None),
            P("col", "row"),
            P("col", "row"),
        ),
        out_specs=(P(None, ("col", "row")), P(), P(None, ("col", "row"))),
        check_vma=False,
    )
```

time: 1430 us -> 143 us (0.10)
  waiting for transfers between devices: 572 us -> 0 us
  other arithmetic: 410 us -> 0 us
  blocking collectives: 286 us -> 0 us
  Pallas kernels: 0 us -> 135 us
  loops' own time: 107 us -> 0 us
  matrix products: 21.8 us -> 0 us
    reduce_scatter x4 -> x0, waiting for transfers between devices: 470 us -> none  [the longest x1 192 us: per_device(): lax.psum_scatter(backward, 'col', scatter_dimension=1, tiled=True)]
    reduce_sum x816 -> x0, other arithmetic: 240 us -> none  [the longest x128 85.7 us: row_step(): pivot = jnp.sum(row_now * pick)]
    psum x3 -> x0, blocking collectives: 232 us -> none  [the longest x1 79.4 us: per_device(): lax.psum((outer(basis, basis), gram_apply), ('row', 'col'))]
    pallas_call x0 -> x1, Pallas kernels: none -> 135 us  [per_device(): pl.pallas_call(functools.partial(step_kernel, n_row, n_col), out_shape=(j...]
    div x192 -> x0, other arithmetic: 131 us -> none  [the longest x128 87.9 us: row_step(): value = (right_row - jnp.sum(row_now[:, None] * solved, axis=0)) / pivot]
    another operation x9 -> x0, loops' own time: 107 us -> none  [the longest x3 105 us: cholesky_lower(): return lax.fori_loop(0, order_small, column_step, jnp.zeros_like(matrix))]
    all_gather x2 -> x0, waiting for transfers between devices: 102 us -> none  [the longest x1 64.4 us: per_device(): pair_cols = lax.all_gather(paired, 'col', axis=1, tiled=True)]
    all_gather x2 -> x0, blocking collectives: 54.2 us -> none  [the longest x1 34.6 us: per_device(): resid_cols = lax.all_gather(resid, 'col', axis=1, tiled=True)]
  transfers between devices with their start and end apart: 6 -> 0, of which waited for: 6 -> 0; matrix products, arithmetic and copies ran while one was open for 2% -> 0% of each run, Pallas kernels for 0% -> 0%
where the time goes in v1:
time: 143 us
  Pallas kernels  135 us (94%)
  local copies, waits for them, and re-layouts  7.05 us (5%)
    pallas_call x1, Pallas kernels, per_device(): pl.pallas_call(functools.partial(step_kernel, n_row, n_col), out_shape=(j...  135 us
    unnamed x11, local copies, waits for them, and re-layouts  7.05 us

profile of v1, /device:TPU:1, one launch (start us, length us, event | category | flops | bytes accessed | tf_op | source)
XLA Modules:
  0.0 143.0 jit_solution(9307863128566311289)
XLA Ops:
  0.6 0.8 copy.8.cols_s.cols_v
  1.4 0.7 copy.9.live_s.live_v
  2.1 0.0 copy-start
  2.1 2.2 %copy-done = bf16[64,2,128,128]{3,2,1,0:T(8,128)(2,1)S(1)} copy-done((bf16[64,2,128,128]{3,2,1,0:T(8,128)(2,1)S(1)}, bf16[64,2,128,128]{3,2,1,0:T(8,128)(2,1)}, u32[]{:S(2)}) %copy-start) | copy-done | bytes 4194328
  4.3 0.0 copy-start.1
  4.3 0.8 copy-done.1
  5.1 0.0 copy-start.2
  5.1 0.8 copy-done.2
  5.8 135.3 %shard_map.76 = (f32[16,512]{1,0:T(8,128)S(1)}, f32[48,48]{1,0:T(8,128)S(1)}, f32[16,512]{1,0:T(8,128)S(1)}) custom-call(f32[16,512]{1,0:T(8,128)S(1)} %copy-done.1, f32[16,512]{1,0:T(8,128)S(1)} %copy-done.2, bf16[64,2,128,128]{3,2,1,0:T(8,128)(2,1)S(1)} %copy-done, s32[64,2]{1,0:T(8,128)S(1)} %copy.8.cols_s.cols_v, s32[64,1]{1,0:T(8,128)S(1)} %copy.9.live_s.live_v, ...), custom_call_target="tpu_custom_call" | custom-call | tf_op jit(solution)/shard_map/pallas_call | solution.py:424
  141.2 0.6 copy.15
  141.8 0.6 copy.16
  142.4 0.6 copy.17
Async XLA Ops:
  2.1 2.2 %copy-start = (bf16[64,2,128,128]{3,2,1,0:T(8,128)(2,1)S(1)}, bf16[64,2,128,128]{3,2,1,0:T(8,128)(2,1)}, u32[]{:S(2)}) copy-start(bf16[64,2,128,128]{3,2,1,0:T(8,128)(2,1)} %blocks_hbm.1) | copy-start | bytes 12582916
  4.3 0.8 copy-start.1
  5.1 0.8 copy-start.2

commit v2 on v0

v2 whole, which is shorter than its diff:
```python
import functools
import math

import jax
import jax.numpy as jnp
from jax import lax
from jax.experimental import pallas as pl
from jax.experimental.pallas import tpu as pltpu
from jax.sharding import PartitionSpec as P

MESH = pl.DeviceIdType.MESH
F32 = jnp.float32
BF16 = jnp.bfloat16
LANES = 128
NT = (((1,), (1,)), ((), ()))
NN = (((1,), (0,)), ((), ()))

AGX_ROW, AGX_COL, AGP_ROW, AGP_COL, AGR_ROW, AGR_COL, RS_ROW, RS_COL = range(0, 16, 2)
AR1, AR2, AR3 = 16, 19, 22
STAGES = 25


def mm(left, right, dims=NN):
    return lax.dot_general(
        left, right, dims, precision=lax.Precision.HIGHEST, preferred_element_type=F32
    )


def fast_mm(left, right, dims=NN):
    return lax.dot_general(left, right, dims, preferred_element_type=F32)


def split_rows(value):
    high = value.astype(BF16)
    low = (value - high.astype(F32)).astype(BF16)
    return jnp.concatenate([high, low], axis=0)


def pad_rows(value, rows):
    return jnp.concatenate(
        [value, jnp.zeros((rows - value.shape[0], value.shape[1]), value.dtype)], axis=0
    )


def lanes_of(rows):
    return lax.broadcasted_iota(jnp.int32, (rows, LANES), 1)


def subs_of(rows):
    return lax.broadcasted_iota(jnp.int32, (rows, LANES), 0)


def eliminate(work, begin, end):
    rows = work.shape[0]
    lane, sub = lanes_of(rows), subs_of(rows)

    def step(k, work):
        row = jnp.sum(jnp.where(sub == k, work, 0.0), axis=0, keepdims=True)
        col = jnp.sum(jnp.where(lane == k, work, 0.0), axis=1, keepdims=True)
        pivot = jnp.sum(jnp.where(lane[:1] == k, row, 0.0), axis=1, keepdims=True)
        inverse = 1.0 / jnp.sqrt(pivot)
        row = row * inverse
        col = col * inverse
        return jnp.where(sub == k, row, jnp.where(sub > k, work - col * row, work))

    return lax.fori_loop(begin, end, step, work)


def symmetric(value):
    return value + pad_rows(value, LANES).T[: value.shape[0]]


def band(value, start, stop, shift=0):
    lane = lanes_of(value.shape[0])
    kept = jnp.where((lane >= start) & (lane < stop), value, 0.0)
    return pltpu.roll(kept, shift % LANES, 1) if shift % LANES else kept


def step_kernel(
    n_row,
    n_col,
    x_hbm,
    p_hbm,
    blocks_hbm,
    cols_s,
    live_s,
    cols_v,
    live_v,
    next_ref,
    reduced_ref,
    resid_ref,
    blk,
    x_ref,
    p_ref,
    rpx,
    cpx,
    rpp,
    cpp,
    rpr,
    cpr,
    prod,
    spread,
    fs,
    fp,
    ra_row,
    rb_row,
    ra_col,
    rb_col,
    sum_row,
    sum_col,
    sum_quad,
    send_sem,
    recv_sem,
    fetch_sem,
):
    me = {"row": lax.axis_index("row"), "col": lax.axis_index("col")}
    sizes = {"row": n_row, "col": n_col}
    me_r, me_c = me["row"], me["col"]
    twin = {axis: me[axis] + 1 - 2 * lax.rem(me[axis], 2) for axis in me}
    width, span = x_hbm.shape
    per = span // LANES
    nb = blocks_hbm.shape[0]
    ncb = per * n_col
    slots = 2 * nb
    order_total = span * n_row * n_col
    pending = []

    def copy_to(axis, stage, mark, src, dst, peer):
        return pltpu.make_async_remote_copy(
            src_ref=src,
            dst_ref=dst,
            send_sem=send_sem.at[stage, mark[0]],
            recv_sem=recv_sem.at[stage, mark[1]],
            device_id=peer if isinstance(peer, dict) else {axis: peer},
            device_id_type=MESH,
        )

    def alike(axis, first, body, carry=0, base=None):
        n = sizes[axis]
        base = me[axis] if base is None else base
        return lax.fori_loop(
            first, n // 2, lambda d, c: body(lax.rem(base + 2 * d, n), c), carry
        )

    def plain(body):
        def run(i, c):
            body(i)
            return c

        return run

    def gather_begin(axis, stage, buf):
        own = buf.at[me[axis]]

        def to_peer(peer):
            return copy_to(axis, stage, (peer, me[axis]), own, own, peer)

        alike(axis, 1, plain(lambda peer: to_peer(peer).start()))
        to_peer(twin[axis]).start()
        pending.append(lambda: alike(axis, 1, plain(lambda peer: to_peer(peer).wait_send())))
        pending.append(lambda: to_peer(twin[axis]).wait_send())

    def gather_relay(axis, stage, buf):
        def onward(slot):
            part = buf.at[slot]
            return copy_to(axis, stage + 1, (slot, slot), part, part, twin[axis])

        def relay(source):
            part = buf.at[source]
            copy_to(axis, stage, (source, source), part, part, source).wait_recv()
            onward(source).start()

        alike(axis, 1, plain(relay))
        pending.append(lambda: alike(axis, 1, plain(lambda slot: onward(slot).wait_send())))

    def gather_finish(axis, stage, buf):
        def landed(slot):
            part = buf.at[slot]
            copy_to(axis, stage + 1, (slot, slot), part, part, twin[axis]).wait_recv()

        other = twin[axis]
        part = buf.at[other]
        copy_to(axis, stage, (other, other), part, part, other).wait_recv()
        alike(axis, 1, plain(landed), base=other)

    def scatter_begin(axis, stage, piece, first):
        def to_twin(dest):
            return copy_to(
                axis, stage, (dest, dest), piece(dest), first.at[dest // 2], twin[axis]
            )

        alike(axis, 0, plain(lambda dest: to_twin(dest).start()), base=twin[axis])
        pending.append(
            lambda: alike(axis, 0, plain(lambda dest: to_twin(dest).wait_send()), base=twin[axis])
        )

    def from_twin(axis, stage, piece, first, dest):
        copy_to(
            axis, stage, (dest, dest), piece(dest), first.at[dest // 2], twin[axis]
        ).wait_recv()
        return piece(dest)[...] + first[dest // 2]

    def scatter_relay(axis, stage, piece, first, second):
        def to_owner(dest):
            return copy_to(
                axis, stage + 1, (dest, me[axis]), piece(dest), second.at[me[axis] // 2], dest
            )

        def relay(dest):
            piece(dest)[...] = from_twin(axis, stage, piece, first, dest)
            to_owner(dest).start()

        alike(axis, 1, plain(relay))
        pending.append(lambda: alike(axis, 1, plain(lambda dest: to_owner(dest).wait_send())))

    def scatter_finish(axis, stage, piece, first, second):
        total = from_twin(axis, stage, piece, first, me[axis])

        def add(source, total):
            part = second.at[source // 2]
            copy_to(axis, stage + 1, (source, source), part, part, source).wait_recv()
            return total + second[source // 2]

        return alike(axis, 1, add, total)

    quad = 2 * lax.rem(me_r, 2) + lax.rem(me_c, 2)

    def others():
        for dr, dc in ((1, 0), (0, 1), (1, 1)):
            row = twin["row"] if dr else me_r
            col = twin["col"] if dc else me_c
            yield {"row": row, "col": col}, 2 * lax.rem(row, 2) + lax.rem(col, 2)

    def sum_axis_begin(axis, stage, buf, value):
        own = buf.at[me[axis] // 2]
        own[...] = value

        def to_peer(peer):
            return copy_to(axis, stage, (peer, me[axis]), own, own, peer)

        alike(axis, 1, plain(lambda peer: to_peer(peer).start()))
        pending.append(lambda: alike(axis, 1, plain(lambda peer: to_peer(peer).wait_send())))

    def sum_axis_end(axis, stage, buf):
        def landed(source):
            part = buf.at[source // 2]
            copy_to(axis, stage, (source, source), part, part, source).wait_recv()

        alike(axis, 1, plain(landed))
        total = buf[0]
        for i in range(1, sizes[axis] // 2):
            total = total + buf[i]
        return total

    def sum_begin(which, base, value):
        sum_axis_begin("row", base, sum_row.at[which], value)

    def sum_second(which, base):
        total = sum_axis_end("row", base, sum_row.at[which])
        sum_axis_begin("col", base + 1, sum_col.at[which], total)

    def sum_third(which, base):
        buf = sum_quad.at[which]
        own = buf.at[quad]
        own[...] = sum_axis_end("col", base + 1, sum_col.at[which])
        for peer, place in others():
            copy = copy_to(None, base + 2, (place, quad), own, own, peer)
            copy.start()
            pending.append(copy.wait_send)

    def sum_end(which, base):
        buf = sum_quad.at[which]
        for peer, place in others():
            part = buf.at[place]
            copy_to(None, base + 2, (place, place), part, part, peer).wait_recv()
        return (buf[0] + buf[1]) + (buf[2] + buf[3])

    fetch = pltpu.make_async_copy(blocks_hbm, blk, fetch_sem.at[0])
    fetch_x = pltpu.make_async_copy(x_hbm, x_ref, fetch_sem.at[1])
    fetch_p = pltpu.make_async_copy(p_hbm, p_ref, fetch_sem.at[2])
    fetch_x.start()
    fetch_p.start()
    barrier = pltpu.get_barrier_semaphore()

    def greet(peer):
        pl.semaphore_signal(barrier, inc=1, device_id=peer, device_id_type=MESH)

    for axis in ("row", "col"):
        alike(axis, 1, plain(lambda peer, axis=axis: greet({axis: peer})))
    for peer, _ in others():
        greet(peer)
    fetch.start()

    fetch_x.wait()
    fetch_p.wait()
    x_now = x_ref[...]
    p_now = p_ref[...]
    for o in range(per):
        rpx[me_r, o] = x_now[:, o * LANES : (o + 1) * LANES]
        cpx[me_c, o] = x_now[:, o * LANES : (o + 1) * LANES]
        rpp[me_r, o] = p_now[:, o * LANES : (o + 1) * LANES]
        cpp[me_c, o] = p_now[:, o * LANES : (o + 1) * LANES]
    pl.semaphore_wait(barrier, n_row // 2 + n_col // 2 + 1)

    gather_begin("row", AGX_ROW, rpx)
    gather_begin("col", AGX_COL, cpx)
    gather_begin("row", AGP_ROW, rpp)
    gather_begin("col", AGP_COL, cpp)

    row_step = per * n_row
    place = cols_v[...] // row_step * per + cols_v[...] % per
    hot = []
    for k in range(2):
        weight = jnp.where(live_v[...] > k, 0.5, 0.0)
        match = lax.broadcasted_iota(jnp.int32, (ncb, nb), 0) == place[k : k + 1]
        hot.append(jnp.where(match, weight, 0.0))
    hot = jnp.concatenate(hot + hot, axis=1).astype(BF16)
    gap = jnp.zeros((width, span), F32)
    gaps = jnp.zeros((LANES - 4 * width, span), F32)
    gram_x = mm(x_now, jnp.concatenate([x_now, gap, p_now, gap, gaps], axis=0), NT)
    gram_p = mm(p_now, jnp.concatenate([gap, gap, gap, p_now, gaps], axis=0), NT)

    def pair_of(b):
        return jnp.concatenate([blk[b, 0], blk[b, 1]], axis=1)

    def flat(panel, r):
        return jnp.concatenate([panel[r, o] for o in range(per)], axis=1)

    def backward(panel):
        def group(r):
            for o in range(per):
                b = r * per + o
                out = fast_mm(split_rows(panel[r, o]), pair_of(b))
                out = out[:width] + out[width:]
                for k in range(2):
                    start = pl.multiple_of((k * nb + b) * width, width)
                    prod[pl.ds(start, width), :] = out[:, k * LANES : (k + 1) * LANES]

        lax.fori_loop(0, n_row, plain(group), 0)
        for vec in range(width):
            part = split_rows(prod[pl.ds(vec, slots, stride=width), :])
            spread[pl.ds(vec, ncb, stride=width), :] = fast_mm(hot, part)

    def forward_group(panel, r):
        outs = []
        for o in range(per):
            b = r * per + o
            picked = []
            for k in range(2):
                g = cols_s[k, b]
                weight = jnp.where(live_s[0, b] > k, 0.5, 0.0)
                picked.append(panel[g // row_step, g % per] * weight)
            out = fast_mm(split_rows(jnp.concatenate(picked, axis=1)), pair_of(b), NT)
            outs.append(out[:width] + out[width:])
        return outs

    def bilinear(left, right):
        high = left.astype(BF16)
        low = (left - high.astype(F32)).astype(BF16)
        rows = jnp.concatenate([high, low], axis=0)
        r_high = right.astype(BF16)
        r_low = (right - r_high.astype(F32)).astype(BF16)
        return fast_mm(
            jnp.concatenate([rows, rows], axis=1), jnp.concatenate([r_high, r_low], axis=1), NT
        )

    def fs_piece(i):
        return fs.at[i]

    def spread_piece(i):
        size = per * width
        return spread.at[pl.ds(pl.multiple_of(i * size, size), size), :]

    gather_relay("row", AGX_ROW, rpx)
    gather_relay("col", AGX_COL, cpx)
    fetch.wait()
    gather_finish("row", AGX_ROW, rpx)
    backward(rpx)
    scatter_begin("col", RS_COL, spread_piece, ra_col)
    gather_finish("col", AGX_COL, cpx)

    def first_group(r, total):
        outs = forward_group(cpx, r)
        for o in range(per):
            fs[r, o * width : (o + 1) * width, :] = outs[o]
        right = jnp.concatenate([gap, jnp.concatenate(outs, axis=1), gap, gap, gaps], axis=0)
        return total + bilinear(flat(rpx, r), right)

    own_xx = lax.fori_loop(0, n_row, first_group, jnp.zeros((2 * width, LANES), F32))
    scatter_begin("row", RS_ROW, fs_piece, ra_row)
    scatter_relay("col", RS_COL, spread_piece, ra_col, rb_col)
    sum_begin(0, AR1, gram_x + gram_p + (own_xx[:width] + own_xx[width:]))
    scatter_relay("row", RS_ROW, fs_piece, ra_row, rb_row)
    sum_second(0, AR1)
    gather_relay("row", AGP_ROW, rpp)
    sum_third(0, AR1)
    gather_relay("col", AGP_COL, cpp)
    row_x = sum_end(0, AR1)

    lane, sub = lanes_of(width), subs_of(width)
    half_xx = band(row_x, width, 2 * width, -width)
    cross = symmetric(half_xx)
    work = band(row_x, 0, width) + pltpu.roll(cross, 64, 1)
    work = eliminate(work + jnp.where(lane == sub + 96, 1.0, 0.0), 0, width)
    halfway = band(work, 64, 64 + width, -64)
    inverse = band(work, 96, 96 + width, -96)
    coef_t = mm(pad_rows(halfway, LANES).T[:width], pad_rows(inverse, LANES))
    moved = mm(coef_t, pad_rows(x_now, LANES))

    image = scatter_finish("row", RS_ROW, fs_piece, ra_row, rb_row)
    image = image + scatter_finish("col", RS_COL, spread_piece, ra_col, rb_col)
    image = jnp.concatenate([image[o * width : (o + 1) * width] for o in range(per)], axis=1)
    resid = image - moved
    for o in range(per):
        rpr[me_r, o] = resid[:, o * LANES : (o + 1) * LANES]
        cpr[me_c, o] = resid[:, o * LANES : (o + 1) * LANES]
    gather_begin("col", AGR_COL, cpr)
    gather_begin("row", AGR_ROW, rpr)
    resid_ref[...] = resid

    gram_r = mm(resid, jnp.concatenate([x_now, resid, p_now, image, gaps], axis=0), NT)
    right = jnp.concatenate([gap, gap, gap, gap, p_now, gaps[width:]], axis=0)
    sum_begin(1, AR2, gram_r + mm(image, right, NT))
    gather_finish("row", AGP_ROW, rpp)
    gather_finish("col", AGP_COL, cpp)

    def second_group(r):
        outs = forward_group(cpp, r)
        fp[r] = jnp.concatenate(outs, axis=1)

    lax.fori_loop(0, n_row, plain(second_group), 0)
    gather_relay("row", AGR_ROW, rpr)
    gather_relay("col", AGR_COL, cpr)
    sum_second(1, AR2)
    gather_finish("row", AGR_ROW, rpr)
    gather_finish("col", AGR_COL, cpr)
    sum_third(1, AR2)

    def third_group(r, total):
        outs = forward_group(cpr, r)
        right = jnp.concatenate([gap, jnp.concatenate(outs, axis=1), fp[r], gap, gaps], axis=0)
        left = jnp.concatenate([flat(rpr, r), flat(rpp, r)], axis=0)
        return total + bilinear(left, right)

    own = lax.fori_loop(0, n_row, third_group, jnp.zeros((4 * width, LANES), F32))
    own = own[: 2 * width] + own[2 * width :]
    sum_begin(2, AR3, own[:width] + pltpu.roll(own[width:], 64, 1))

    full = 3 * width
    row_r = sum_end(1, AR2)
    lane, sub = lanes_of(full), subs_of(full)
    row_p = band(row_x, 3 * width, 4 * width, -width)
    gram = jnp.concatenate(
        [
            0.5 * band(row_x, 0, width) + band(row_x, 2 * width, full),
            band(row_r, 0, width) + 0.5 * band(row_r, width, 2 * width) + band(row_r, 2 * width, full),
            0.5 * row_p,
        ],
        axis=0,
    )
    edge = jnp.zeros((width, LANES), F32)
    known = symmetric(
        jnp.concatenate(
            [half_xx + band(row_r, 64, 64 + width, -32), band(row_r, full, full + width, -full), edge],
            axis=0,
        )
    )
    work = symmetric(gram) + jnp.where(lane == sub + 64, 1.0, 0.0)
    work = eliminate(work, 0, width)
    sum_second(2, AR3)
    work = eliminate(work, width, 2 * width)
    sum_third(2, AR3)
    work = eliminate(work, 2 * width, full)
    inverse = band(work, 64, 64 + full, -64)
    inverse_pad = pad_rows(inverse, LANES)

    last = sum_end(2, AR3)
    late = jnp.concatenate([edge, band(last, 0, full), band(last, 64, 64 + full, -64)], axis=0)
    middle = known + symmetric(late)

    reduced = mm(mm(inverse, pad_rows(middle, LANES)), inverse_pad, NT)
    reduced_ref[...] = reduced[:, :full]
    shifted = reduced + jnp.where(lane == sub, 3.0, 0.0)
    target_t = mm(shifted[:width], pad_rows(shifted, LANES))
    mixing_t = mm(target_t, inverse_pad)
    gram_new = mm(target_t, pad_rows(target_t, LANES), NT)
    work = band(gram_new, 0, width) + pltpu.roll(mixing_t, 64, 1)
    work = eliminate(work, 0, width)
    final = band(work, 64, 64 + full, -64) * math.sqrt(order_total)
    next_ref[...] = mm(final, pad_rows(jnp.concatenate([x_now, resid, p_now], axis=0), LANES))

    for leave in pending:
        leave()


def per_device(block_vecs, direction, blocks, block_cols, live_counts):
    n_row = lax.axis_size("row")
    n_col = lax.axis_size("col")
    width, span = block_vecs.shape
    per = span // LANES
    nb = blocks.shape[0]
    vmem = pl.BlockSpec(memory_space=pltpu.VMEM)
    smem = pl.BlockSpec(memory_space=pltpu.SMEM)
    hbm = pl.BlockSpec(memory_space=pltpu.HBM)
    block_cols, live_counts = block_cols.T, live_counts.T
    row_panel = pltpu.VMEM((n_row, per, width, LANES), F32)
    col_panel = pltpu.VMEM((n_col, per, width, LANES), F32)
    row_half = pltpu.VMEM((n_row // 2, per * width, LANES), F32)
    col_half = pltpu.VMEM((n_col // 2, per * width, LANES), F32)
    peers = max(n_row, n_col)
    return pl.pallas_call(
        functools.partial(step_kernel, n_row, n_col),
        out_shape=(
            jax.ShapeDtypeStruct((width, span), F32),
            jax.ShapeDtypeStruct((3 * width, 3 * width), F32),
            jax.ShapeDtypeStruct((width, span), F32),
        ),
        in_specs=[hbm, hbm, hbm, smem, smem, vmem, vmem],
        out_specs=(vmem, vmem, vmem),
        scratch_shapes=[
            pltpu.VMEM(blocks.shape, blocks.dtype),
            pltpu.VMEM((width, span), F32),
            pltpu.VMEM((width, span), F32),
            *([row_panel, col_panel] * 3),
            pltpu.VMEM((2 * nb * width, LANES), F32),
            pltpu.VMEM((n_col * per * width, LANES), F32),
            pltpu.VMEM((n_row, per * width, LANES), F32),
            pltpu.VMEM((n_row, width, span), F32),
            row_half,
            row_half,
            col_half,
            col_half,
            pltpu.VMEM((3, n_row // 2, width, LANES), F32),
            pltpu.VMEM((3, n_col // 2, width, LANES), F32),
            pltpu.VMEM((3, 4, width, LANES), F32),
            pltpu.SemaphoreType.DMA((STAGES, peers)),
            pltpu.SemaphoreType.DMA((STAGES, peers)),
            pltpu.SemaphoreType.DMA((3,)),
        ],
        compiler_params=pltpu.CompilerParams(
            collective_id=0, has_side_effects=True, vmem_limit_bytes=63 * 2**20
        ),
    )(block_vecs, direction, blocks, block_cols, live_counts, block_cols, live_counts)


def solution(mesh):
    return jax.shard_map(
        per_device,
        mesh=mesh,
        in_specs=(
            P(None, ("col", "row")),
            P(None, ("col", "row")),
            P("col", "row", None, None),
            P("col", "row"),
            P("col", "row"),
        ),
        out_specs=(P(None, ("col", "row")), P(), P(None, ("col", "row"))),
        check_vma=False,
    )
```

time: 1430 us -> 101 us (0.07)
  waiting for transfers between devices: 572 us -> 0 us
  other arithmetic: 410 us -> 0 us
  blocking collectives: 286 us -> 0 us
  loops' own time: 107 us -> 0 us
  Pallas kernels: 0 us -> 95.7 us
  matrix products: 21.8 us -> 0 us
    reduce_scatter x4 -> x0, waiting for transfers between devices: 470 us -> none  [the longest x1 192 us: per_device(): lax.psum_scatter(backward, 'col', scatter_dimension=1, tiled=True)]
    reduce_sum x816 -> x0, other arithmetic: 240 us -> none  [the longest x128 85.7 us: row_step(): pivot = jnp.sum(row_now * pick)]
    psum x3 -> x0, blocking collectives: 232 us -> none  [the longest x1 79.4 us: per_device(): lax.psum((outer(basis, basis), gram_apply), ('row', 'col'))]
    div x192 -> x0, other arithmetic: 131 us -> none  [the longest x128 87.9 us: row_step(): value = (right_row - jnp.sum(row_now[:, None] * solved, axis=0)) / pivot]
    another operation x9 -> x0, loops' own time: 107 us -> none  [the longest x3 105 us: cholesky_lower(): return lax.fori_loop(0, order_small, column_step, jnp.zeros_like(matrix))]
    all_gather x2 -> x0, waiting for transfers between devices: 102 us -> none  [the longest x1 64.4 us: per_device(): pair_cols = lax.all_gather(paired, 'col', axis=1, tiled=True)]
    pallas_call x0 -> x1, Pallas kernels: none -> 95.7 us  [per_device(): pl.pallas_call(functools.partial(step_kernel, n_row, n_col), out_shape=(j...]
    all_gather x2 -> x0, blocking collectives: 54.2 us -> none  [the longest x1 34.6 us: per_device(): resid_cols = lax.all_gather(resid, 'col', axis=1, tiled=True)]
  transfers between devices with their start and end apart: 6 -> 0, of which waited for: 6 -> 0; matrix products, arithmetic and copies ran while one was open for 2% -> 0% of each run, Pallas kernels for 0% -> 0%
where the time goes in v2:
time: 101 us; the launch traced here: 100 us
  Pallas kernels  95.7 us (95%)
  local copies, waits for them, and re-layouts  4.09 us (4%)
    pallas_call x1, Pallas kernels, per_device(): pl.pallas_call(functools.partial(step_kernel, n_row, n_col), out_shape=(j...  95.7 us
    unnamed x3, local copies, waits for them, and re-layouts  4.09 us

profile of v2, /device:TPU:1, one launch (start us, length us, event | category | flops | bytes accessed | tf_op | source)
XLA Modules:
  0.0 100.5 jit_solution(14203530359909729062)
XLA Ops:
  0.6 95.7 %shard_map.76 = (f32[16,512]{1,0:T(8,128)}, f32[48,48]{1,0:T(8,128)}, f32[16,512]{1,0:T(8,128)}) custom-call(f32[16,512]{1,0:T(8,128)} %x_hbm.1, f32[16,512]{1,0:T(8,128)} %p_hbm.1, bf16[64,2,128,128]{3,2,1,0:T(8,128)(2,1)} %blocks_hbm.1, s32[2,64]{1,0:T(2,128)} %bitcast.2, s32[1,64]{1,0:T(1,128)} %bitcast.4, s32[2,64]{1,0:T(2,128)} %bitcast.3, s32[1,64]{1,0:T(1,128)} %bitcast.5), custom_call_target="tpu_custom_call" | custom-call | tf_op jit(solution)/shard_map/pallas_call | solution.py:511
  96.4 1.4 %copy.11 = f32[16,512]{1,0:T(8,128)} copy(f32[16,512]{1,0:T(8,128)} %get-tuple-element.6) | data formatting | bytes 65536
  97.7 1.3 %copy.12 = f32[48,48]{1,0:T(8,128)} copy(f32[48,48]{1,0:T(8,128)} %get-tuple-element.7) | data formatting | bytes 18432
  99.1 1.4 %copy.13 = f32[16,512]{1,0:T(8,128)} copy(f32[16,512]{1,0:T(8,128)} %get-tuple-element.8) | data formatting | bytes 65536

commit v3 on v2

--- a/solution.py
+++ b/solution.py
@@ -111,6 +111,7 @@
     sum_quad,
     send_sem,
     recv_sem,
+    each_sem,
     fetch_sem,
 ):
     me = {"row": lax.axis_index("row"), "col": lax.axis_index("col")}
@@ -125,15 +126,19 @@
     order_total = span * n_row * n_col
     pending = []
 
-    def copy_to(axis, stage, mark, src, dst, peer):
+    def copy_to(axis, stage, src, dst, peer, single=None):
         return pltpu.make_async_remote_copy(
             src_ref=src,
             dst_ref=dst,
-            send_sem=send_sem.at[stage, mark[0]],
-            recv_sem=recv_sem.at[stage, mark[1]],
+            send_sem=send_sem.at[stage],
+            recv_sem=recv_sem.at[stage] if single is None else each_sem.at[stage // 2, single],
             device_id=peer if isinstance(peer, dict) else {axis: peer},
             device_id_type=MESH,
         )
+
+    def whole(stage, buf, count):
+        part = buf.at[pl.ds(0, count)]
+        return copy_to("row", stage, part, part, twin["row"])
 
     def alike(axis, first, body, carry=0, base=None):
         n = sizes[axis]
@@ -151,102 +156,75 @@
 
     def gather_begin(axis, stage, buf):
         own = buf.at[me[axis]]
-
-        def to_peer(peer):
-            return copy_to(axis, stage, (peer, me[axis]), own, own, peer)
-
-        alike(axis, 1, plain(lambda peer: to_peer(peer).start()))
-        to_peer(twin[axis]).start()
-        pending.append(lambda: alike(axis, 1, plain(lambda peer: to_peer(peer).wait_send())))
-        pending.append(lambda: to_peer(twin[axis]).wait_send())
+        half = sizes[axis] // 2
+        alike(
+            axis,
+            1,
+            plain(lambda peer: copy_to(axis, stage, own, own, peer, me[axis] // 2).start()),
+        )
+        copy_to(axis, stage + 1, own, own, twin[axis]).start()
+        if half > 1:
+            pending.append(lambda: whole(stage, buf, half - 1).wait_send())
+        pending.append(lambda: whole(stage + 1, buf, half).wait_send())
 
     def gather_relay(axis, stage, buf):
-        def onward(slot):
-            part = buf.at[slot]
-            return copy_to(axis, stage + 1, (slot, slot), part, part, twin[axis])
-
         def relay(source):
             part = buf.at[source]
-            copy_to(axis, stage, (source, source), part, part, source).wait_recv()
-            onward(source).start()
+            copy_to(axis, stage, part, part, source, source // 2).wait_recv()
+            copy_to(axis, stage + 1, part, part, twin[axis]).start()
 
         alike(axis, 1, plain(relay))
-        pending.append(lambda: alike(axis, 1, plain(lambda slot: onward(slot).wait_send())))
 
     def gather_finish(axis, stage, buf):
-        def landed(slot):
-            part = buf.at[slot]
-            copy_to(axis, stage + 1, (slot, slot), part, part, twin[axis]).wait_recv()
-
-        other = twin[axis]
-        part = buf.at[other]
-        copy_to(axis, stage, (other, other), part, part, other).wait_recv()
-        alike(axis, 1, plain(landed), base=other)
+        whole(stage + 1, buf, sizes[axis] // 2).wait_recv()
 
     def scatter_begin(axis, stage, piece, first):
         def to_twin(dest):
-            return copy_to(
-                axis, stage, (dest, dest), piece(dest), first.at[dest // 2], twin[axis]
-            )
-
-        alike(axis, 0, plain(lambda dest: to_twin(dest).start()), base=twin[axis])
-        pending.append(
-            lambda: alike(axis, 0, plain(lambda dest: to_twin(dest).wait_send()), base=twin[axis])
-        )
+            copy_to(
+                axis, stage, piece(dest), first.at[dest // 2], twin[axis], dest // 2
+            ).start()
+
+        alike(axis, 0, plain(to_twin), base=twin[axis])
+        pending.append(lambda: whole(stage, first, sizes[axis] // 2).wait_send())
 
     def from_twin(axis, stage, piece, first, dest):
-        copy_to(
-            axis, stage, (dest, dest), piece(dest), first.at[dest // 2], twin[axis]
-        ).wait_recv()
+        part = first.at[dest // 2]
+        copy_to(axis, stage, part, part, twin[axis], dest // 2).wait_recv()
         return piece(dest)[...] + first[dest // 2]
 
     def scatter_relay(axis, stage, piece, first, second):
-        def to_owner(dest):
-            return copy_to(
-                axis, stage + 1, (dest, me[axis]), piece(dest), second.at[me[axis] // 2], dest
-            )
-
         def relay(dest):
             piece(dest)[...] = from_twin(axis, stage, piece, first, dest)
-            to_owner(dest).start()
+            copy_to(axis, stage + 1, piece(dest), second.at[me[axis] // 2], dest).start()
 
         alike(axis, 1, plain(relay))
-        pending.append(lambda: alike(axis, 1, plain(lambda dest: to_owner(dest).wait_send())))
+        if sizes[axis] > 2:
+            pending.append(lambda: whole(stage + 1, second, sizes[axis] // 2 - 1).wait_send())
 
     def scatter_finish(axis, stage, piece, first, second):
         total = from_twin(axis, stage, piece, first, me[axis])
-
-        def add(source, total):
-            part = second.at[source // 2]
-            copy_to(axis, stage + 1, (source, source), part, part, source).wait_recv()
-            return total + second[source // 2]
-
-        return alike(axis, 1, add, total)
+        if sizes[axis] > 2:
+            whole(stage + 1, second, sizes[axis] // 2 - 1).wait_recv()
+        return alike(axis, 1, lambda source, total: total + second[source // 2], total)
 
     quad = 2 * lax.rem(me_r, 2) + lax.rem(me_c, 2)
 
     def others():
-        for dr, dc in ((1, 0), (0, 1), (1, 1)):
+        for dr, dc in ((1, 1), (0, 1), (1, 0)):
             row = twin["row"] if dr else me_r
             col = twin["col"] if dc else me_c
-            yield {"row": row, "col": col}, 2 * lax.rem(row, 2) + lax.rem(col, 2)
+            yield {"row": row, "col": col}
 
     def sum_axis_begin(axis, stage, buf, value):
         own = buf.at[me[axis] // 2]
         own[...] = value
-
-        def to_peer(peer):
-            return copy_to(axis, stage, (peer, me[axis]), own, own, peer)
-
-        alike(axis, 1, plain(lambda peer: to_peer(peer).start()))
-        pending.append(lambda: alike(axis, 1, plain(lambda peer: to_peer(peer).wait_send())))
+        alike(axis, 1, plain(lambda peer: copy_to(axis, stage, own, own, peer).start()))
+        if sizes[axis] > 2:
+            pending.append(lambda: whole(stage, buf, sizes[axis] // 2 - 1).wait_send())
 
     def sum_axis_end(axis, stage, buf):
-        def landed(source):
-            part = buf.at[source // 2]
-            copy_to(axis, stage, (source, source), part, part, source).wait_recv()
-
-        alike(axis, 1, plain(landed))
+        if sizes[axis] > 2:
+            whole(stage, buf, sizes[axis] // 2 - 1).wait_recv()
         total = buf[0]
         for i in range(1, sizes[axis] // 2):
             total = total + buf[i]
@@ -263,16 +241,13 @@
         buf = sum_quad.at[which]
         own = buf.at[quad]
         own[...] = sum_axis_end("col", base + 1, sum_col.at[which])
-        for peer, place in others():
-            copy = copy_to(None, base + 2, (place, quad), own, own, peer)
-            copy.start()
-            pending.append(copy.wait_send)
+        for peer in others():
+            copy_to(None, base + 2, own, own, peer).start()
+        pending.append(lambda: whole(base + 2, buf, 3).wait_send())
 
     def sum_end(which, base):
         buf = sum_quad.at[which]
-        for peer, place in others():
-            part = buf.at[place]
-            copy_to(None, base + 2, (place, place), part, part, peer).wait_recv()
+        whole(base + 2, buf, 3).wait_recv()
         return (buf[0] + buf[1]) + (buf[2] + buf[3])
 
     fetch = pltpu.make_async_copy(blocks_hbm, blk, fetch_sem.at[0])
@@ -287,7 +262,7 @@
 
     for axis in ("row", "col"):
         alike(axis, 1, plain(lambda peer, axis=axis: greet({axis: peer})))
-    for peer, _ in others():
+    for peer in others():
         greet(peer)
     fetch.start()
 
@@ -302,10 +277,8 @@
         cpp[me_c, o] = p_now[:, o * LANES : (o + 1) * LANES]
     pl.semaphore_wait(barrier, n_row // 2 + n_col // 2 + 1)
 
+    gather_begin("col", AGX_COL, cpx)
     gather_begin("row", AGX_ROW, rpx)
-    gather_begin("col", AGX_COL, cpx)
-    gather_begin("row", AGP_ROW, rpp)
-    gather_begin("col", AGP_COL, cpp)
 
     row_step = per * n_row
     place = cols_v[...] // row_step * per + cols_v[...] % per
@@ -373,6 +346,8 @@
 
     gather_relay("row", AGX_ROW, rpx)
     gather_relay("col", AGX_COL, cpx)
+    gather_begin("col", AGP_COL, cpp)
+    gather_begin("row", AGP_ROW, rpp)
     fetch.wait()
     gather_finish("row", AGX_ROW, rpx)
     backward(rpx)
@@ -533,8 +508,9 @@
             pltpu.VMEM((3, n_row // 2, width, LANES), F32),
             pltpu.VMEM((3, n_col // 2, width, LANES), F32),
             pltpu.VMEM((3, 4, width, LANES), F32),
-            pltpu.SemaphoreType.DMA((STAGES, peers)),
-            pltpu.SemaphoreType.DMA((STAGES, peers)),
+            pltpu.SemaphoreType.DMA((STAGES,)),
+            pltpu.SemaphoreType.DMA((STAGES,)),
+            pltpu.SemaphoreType.DMA((8, peers // 2)),
             pltpu.SemaphoreType.DMA((3,)),
         ],
         compiler_params=pltpu.CompilerParams(

time: 101 us -> 92.3 us (0.914)
  Pallas kernels: 95.7 us -> 87.3 us
    pallas_call x1, Pallas kernels: 95.7 us -> 87.3 us  [per_device(): pl.pallas_call(functools.partial(step_kernel, n_row, n_col), out_shape=(j...]
where the time goes in v3:
time: 92.3 us; the launch traced here: 92 us
  Pallas kernels  87.3 us (95%)
  local copies, waits for them, and re-layouts  4.09 us (4%)
    pallas_call x1, Pallas kernels, per_device(): pl.pallas_call(functools.partial(step_kernel, n_row, n_col), out_shape=(j...  87.3 us
    unnamed x3, local copies, waits for them, and re-layouts  4.09 us

profile of v3, /device:TPU:1, one launch (start us, length us, event | category | flops | bytes accessed | tf_op | source)
XLA Modules:
  0.0 92.0 jit_solution(16884353386466930831)
XLA Ops:
  0.6 87.3 %shard_map.76 = (f32[16,512]{1,0:T(8,128)}, f32[48,48]{1,0:T(8,128)}, f32[16,512]{1,0:T(8,128)}) custom-call(f32[16,512]{1,0:T(8,128)} %x_hbm.1, f32[16,512]{1,0:T(8,128)} %p_hbm.1, bf16[64,2,128,128]{3,2,1,0:T(8,128)(2,1)} %blocks_hbm.1, s32[2,64]{1,0:T(2,128)} %bitcast.2, s32[1,64]{1,0:T(1,128)} %bitcast.4, s32[2,64]{1,0:T(2,128)} %bitcast.3, s32[1,64]{1,0:T(1,128)} %bitcast.5), custom_call_target="tpu_custom_call" | custom-call | tf_op jit(solution)/shard_map/pallas_call | solution.py:486
  87.9 1.4 %copy.11 = f32[16,512]{1,0:T(8,128)} copy(f32[16,512]{1,0:T(8,128)} %get-tuple-element.6) | data formatting | bytes 65536
  89.3 1.3 %copy.12 = f32[48,48]{1,0:T(8,128)} copy(f32[48,48]{1,0:T(8,128)} %get-tuple-element.7) | data formatting | bytes 18432
  90.6 1.4 %copy.13 = f32[16,512]{1,0:T(8,128)} copy(f32[16,512]{1,0:T(8,128)} %get-tuple-element.8) | data formatting | bytes 65536

commit v4 on v3

--- a/solution.py
+++ b/solution.py
@@ -143,9 +143,9 @@
     def alike(axis, first, body, carry=0, base=None):
         n = sizes[axis]
         base = me[axis] if base is None else base
-        return lax.fori_loop(
-            first, n // 2, lambda d, c: body(lax.rem(base + 2 * d, n), c), carry
-        )
+        for d in sorted(range(first, n // 2), key=lambda d: -min(d, n // 2 - d)):
+            carry = body(lax.rem(base + 2 * d, n), carry)
+        return carry
 
     def plain(body):
         def run(i, c):
@@ -363,8 +363,8 @@
 
     own_xx = lax.fori_loop(0, n_row, first_group, jnp.zeros((2 * width, LANES), F32))
     scatter_begin("row", RS_ROW, fs_piece, ra_row)
+    sum_begin(0, AR1, gram_x + gram_p + (own_xx[:width] + own_xx[width:]))
     scatter_relay("col", RS_COL, spread_piece, ra_col, rb_col)
-    sum_begin(0, AR1, gram_x + gram_p + (own_xx[:width] + own_xx[width:]))
     scatter_relay("row", RS_ROW, fs_piece, ra_row, rb_row)
     sum_second(0, AR1)
     gather_relay("row", AGP_ROW, rpp)

time: 92.3 us -> 88.4 us (0.958)
  Pallas kernels: 87.3 us -> 83.3 us
    pallas_call x1, Pallas kernels: 87.3 us -> 83.3 us  [per_device(): pl.pallas_call(functools.partial(step_kernel, n_row, n_col), out_shape=(j...]
where the time goes in v4:
time: 88.4 us; the launch traced here: 88.1 us
  Pallas kernels  83.3 us (94%)
  local copies, waits for them, and re-layouts  4.09 us (5%)
    pallas_call x1, Pallas kernels, per_device(): pl.pallas_call(functools.partial(step_kernel, n_row, n_col), out_shape=(j...  83.3 us
    unnamed x3, local copies, waits for them, and re-layouts  4.09 us

profile of v4, /device:TPU:1, one launch (start us, length us, event | category | flops | bytes accessed | tf_op | source)
XLA Modules:
  0.0 88.1 jit_solution(13550330249535847585)
XLA Ops:
  0.6 83.3 %shard_map.76 = (f32[16,512]{1,0:T(8,128)}, f32[48,48]{1,0:T(8,128)}, f32[16,512]{1,0:T(8,128)}) custom-call(f32[16,512]{1,0:T(8,128)} %x_hbm.1, f32[16,512]{1,0:T(8,128)} %p_hbm.1, bf16[64,2,128,128]{3,2,1,0:T(8,128)(2,1)} %blocks_hbm.1, s32[2,64]{1,0:T(2,128)} %bitcast.2, s32[1,64]{1,0:T(1,128)} %bitcast.4, s32[2,64]{1,0:T(2,128)} %bitcast.3, s32[1,64]{1,0:T(1,128)} %bitcast.5), custom_call_target="tpu_custom_call" | custom-call | tf_op jit(solution)/shard_map/pallas_call | solution.py:486
  84.0 1.4 %copy.11 = f32[16,512]{1,0:T(8,128)} copy(f32[16,512]{1,0:T(8,128)} %get-tuple-element.6) | data formatting | bytes 65536
  85.4 1.3 %copy.12 = f32[48,48]{1,0:T(8,128)} copy(f32[48,48]{1,0:T(8,128)} %get-tuple-element.7) | data formatting | bytes 18432
  86.7 1.4 %copy.13 = f32[16,512]{1,0:T(8,128)} copy(f32[16,512]{1,0:T(8,128)} %get-tuple-element.8) | data formatting | bytes 65536

commit v5 on v4

--- a/solution.py
+++ b/solution.py
@@ -309,7 +309,7 @@
                     start = pl.multiple_of((k * nb + b) * width, width)
                     prod[pl.ds(start, width), :] = out[:, k * LANES : (k + 1) * LANES]
 
-        lax.fori_loop(0, n_row, plain(group), 0)
+        lax.fori_loop(0, n_row, plain(group), 0, unroll=4)
         for vec in range(width):
             part = split_rows(prod[pl.ds(vec, slots, stride=width), :])
             spread[pl.ds(vec, ncb, stride=width), :] = fast_mm(hot, part)
@@ -361,14 +361,14 @@
         right = jnp.concatenate([gap, jnp.concatenate(outs, axis=1), gap, gap, gaps], axis=0)
         return total + bilinear(flat(rpx, r), right)
 
-    own_xx = lax.fori_loop(0, n_row, first_group, jnp.zeros((2 * width, LANES), F32))
+    own_xx = lax.fori_loop(0, n_row, first_group, jnp.zeros((2 * width, LANES), F32), unroll=4)
     scatter_begin("row", RS_ROW, fs_piece, ra_row)
     sum_begin(0, AR1, gram_x + gram_p + (own_xx[:width] + own_xx[width:]))
     scatter_relay("col", RS_COL, spread_piece, ra_col, rb_col)
+    sum_second(0, AR1)
     scatter_relay("row", RS_ROW, fs_piece, ra_row, rb_row)
-    sum_second(0, AR1)
+    sum_third(0, AR1)
     gather_relay("row", AGP_ROW, rpp)
-    sum_third(0, AR1)
     gather_relay("col", AGP_COL, cpp)
     row_x = sum_end(0, AR1)
 
@@ -403,7 +403,7 @@
         outs = forward_group(cpp, r)
         fp[r] = jnp.concatenate(outs, axis=1)
 
-    lax.fori_loop(0, n_row, plain(second_group), 0)
+    lax.fori_loop(0, n_row, plain(second_group), 0, unroll=4)
     gather_relay("row", AGR_ROW, rpr)
     gather_relay("col", AGR_COL, cpr)
     sum_second(1, AR2)
@@ -417,7 +417,7 @@
         left = jnp.concatenate([flat(rpr, r), flat(rpp, r)], axis=0)
         return total + bilinear(left, right)
 
-    own = lax.fori_loop(0, n_row, third_group, jnp.zeros((4 * width, LANES), F32))
+    own = lax.fori_loop(0, n_row, third_group, jnp.zeros((4 * width, LANES), F32), unroll=4)
     own = own[: 2 * width] + own[2 * width :]
     sum_begin(2, AR3, own[:width] + pltpu.roll(own[width:], 64, 1))
 

time: 88.4 us -> 84.8 us (0.959)
  Pallas kernels: 83.3 us -> 79.8 us
    pallas_call x1, Pallas kernels: 83.3 us -> 79.8 us  [per_device(): pl.pallas_call(functools.partial(step_kernel, n_row, n_col), out_shape=(j...]
where the time goes in v5:
time: 84.8 us; the launch traced here: 84.5 us
  Pallas kernels  79.8 us (94%)
  local copies, waits for them, and re-layouts  4.09 us (5%)
    pallas_call x1, Pallas kernels, per_device(): pl.pallas_call(functools.partial(step_kernel, n_row, n_col), out_shape=(j...  79.8 us
    unnamed x3, local copies, waits for them, and re-layouts  4.09 us

profile of v5, /device:TPU:1, one launch (start us, length us, event | category | flops | bytes accessed | tf_op | source)
XLA Modules:
  0.0 84.5 jit_solution(2573055643668475870)
XLA Ops:
  0.6 79.8 %shard_map.76 = (f32[16,512]{1,0:T(8,128)}, f32[48,48]{1,0:T(8,128)}, f32[16,512]{1,0:T(8,128)}) custom-call(f32[16,512]{1,0:T(8,128)} %x_hbm.1, f32[16,512]{1,0:T(8,128)} %p_hbm.1, bf16[64,2,128,128]{3,2,1,0:T(8,128)(2,1)} %blocks_hbm.1, s32[2,64]{1,0:T(2,128)} %bitcast.2, s32[1,64]{1,0:T(1,128)} %bitcast.4, s32[2,64]{1,0:T(2,128)} %bitcast.3, s32[1,64]{1,0:T(1,128)} %bitcast.5), custom_call_target="tpu_custom_call" | custom-call | tf_op jit(solution)/shard_map/pallas_call | solution.py:486
  80.4 1.4 %copy.11 = f32[16,512]{1,0:T(8,128)} copy(f32[16,512]{1,0:T(8,128)} %get-tuple-element.6) | data formatting | bytes 65536
  81.8 1.3 %copy.12 = f32[48,48]{1,0:T(8,128)} copy(f32[48,48]{1,0:T(8,128)} %get-tuple-element.7) | data formatting | bytes 18432
  83.1 1.4 %copy.13 = f32[16,512]{1,0:T(8,128)} copy(f32[16,512]{1,0:T(8,128)} %get-tuple-element.8) | data formatting | bytes 65536
